TPU v7x, 32 devices: a whole 2x2x4 slice. The times are simulated.
32 devices in a mesh: rt: 8 (over y, x, core), ct: 4 (over z).
Axes of the slice: x: 2, y: 2, z: 4, core: 2. Of those that a mesh axis runs over, the one named last changes fastest.
Arguments:
- factor_rows: float32 [48, 2, 1024, 1024], P('rt', None, 'ct'), as said below
- slot_row: int32 [48], replicated, may hold values from -1 to 31, as said below
- known: float32 [48, 1024, 256], P('rt', 'ct'), may hold values from -6 to 6
- rhs: float32 [2, 1024, 256], P(None, 'ct', 'rt'), may hold values from -6 to 6
Outputs:
- solved: float32 [2, 1024, 256], P(None, 'ct', 'rt')
Inputs may be any that keep to these rules, and one draw needn't show every extreme that they name: `slot_row`: each row tile 0 to 31 stands in exactly one slot; the other slots hold -1. The slots of one index of rt are the 6 consecutive ones; at most 6 are live, and some index of rt has all 6 live. `factor_rows`: diagonal tiles L[0, 0] and L[1, 1] are lower triangular with diagonal entries from 1 to 2; the entry block (0, 1) is zero; entries of empty slots are arbitrary.
All inputs are finite; a program needn't handle non-finite values.
Results may differ from a plain program's by a relative error of at most 0.0003.
Values sent between devices are 32-bit elements; how exact they have to be, the bound alone decides.
No kernel may reach another device: no remote copies, remote signals or barrier semaphores. Data moves between devices by JAX's collectives and lax.ppermute only.
A program may use at most 64 MiB of HBM per device.

v0:
```python
import jax
import jax.numpy as jnp
from jax import lax
from jax.sharding import PartitionSpec as P


def spread(value, axis, root):
    mine = lax.axis_index(axis) == root
    return lax.psum(jnp.where(mine, value, jnp.zeros_like(value)), axis)


def shards(factor_rows, slot_row, known, rhs):
    high = lax.Precision.HIGHEST
    band = known.shape[1]
    columns = rhs.shape[2]
    slot_count = factor_rows.shape[0]
    offset = lax.axis_index("ct") * band
    col_offset = lax.axis_index("rt") * columns
    local_rows = lax.dynamic_slice_in_dim(
        slot_row, lax.axis_index("rt") * slot_count, slot_count, 0
    )
    live = (local_rows >= 2).astype(jnp.float32)
    masked = known * live[:, None, None]
    partial_value = jnp.einsum("scka,skr->car", factor_rows, masked, precision=high)
    pick_zero = local_rows == 0
    pick_one = local_rows == 1
    diag_zero = jnp.sum(jnp.where(pick_zero[:, None, None], factor_rows[:, 0], 0.0), 0)
    diag_one = jnp.sum(jnp.where(pick_one[:, None, None], factor_rows[:, 1], 0.0), 0)
    lower_one = jnp.sum(jnp.where(pick_one[:, None, None], factor_rows[:, 0], 0.0), 0)
    owner_zero = jnp.argmax(slot_row == 0) // slot_count
    owner_one = jnp.argmax(slot_row == 1) // slot_count
    tile_zero = spread(diag_zero, "rt", owner_zero)
    tile_one, tile_lower = (spread(diag_one, "rt", owner_one), spread(lower_one, "rt", owner_one))
    total = lax.psum(partial_value, ("rt", "ct"))
    rows_mine = lax.dynamic_slice_in_dim(total, offset, band, 1)
    mine = lax.dynamic_slice_in_dim(rows_mine, col_offset, columns, 2)
    residual = lax.all_gather(rhs - mine, "ct", axis=1, tiled=True)
    whole_zero, whole_one = (
        lax.all_gather(tile_zero, "ct", axis=0, tiled=True),
        lax.all_gather(tile_one, "ct", axis=0, tiled=True),
    )
    solved_one = lax.linalg.triangular_solve(
        whole_one, residual[1], left_side=True, lower=True, transpose_a=True
    )
    one_band = lax.dynamic_slice_in_dim(solved_one, offset, band, 0)
    coupling = jnp.einsum("ka,kr->ar", tile_lower, one_band, precision=high)
    coupled = lax.psum(coupling, "ct")
    solved_zero = lax.linalg.triangular_solve(
        whole_zero, residual[0] - coupled, left_side=True, lower=True, transpose_a=True
    )
    zero_band = lax.dynamic_slice_in_dim(solved_zero, offset, band, 0)
    return jnp.stack([zero_band, one_band])


def solution(mesh):
    in_specs = (P("rt", None, "ct", None), P(), P("rt", "ct", None), P(None, "ct", "rt"))
    out_specs = P(None, "ct", "rt")
    return jax.shard_map(shards, mesh=mesh, in_specs=in_specs, out_specs=out_specs, check_vma=False)
```

profile of v0, /device:TPU:0, one launch (start us, length us, event | category | flops | bytes accessed | tf_op | source)
XLA Modules:
  0.0 562.1 jit_solution(5160775739267857526)
XLA Ops:
  6.5 1.4 compare_reduce_fusion
  10.0 1.4 compare_reduce_fusion.1
  14.2 6.1 %fusion.2 = (f32[256,1024]{1,0:T(8,128)S(1)}, f32[256,1024]{1,0:T(8,128)S(1)}, f32[256,1024]{1,0:T(8,128)S(1)}) fusion(f32[6,2,256,1024]{3,2,1,0:T(8,128)} %param.6, pred[6]{0:T(512)(128)(4,1)S(1)} %get-tuple-element.53, pred[6]{0:T(512)(128)(4,1)S(1)} %get-tuple-element.54), kind=kLoop, calls=%fused_computation.9 | loop fusion | flops 8650752 | bytes 15728652 | tf_op jit(solution)/shard_map/reduce_sum | solution.py:29
  20.3 1.1 broadcast_select_fusion.2
  21.4 1.6 broadcast_select_fusion
  23.3 14.9 %convolution_bitcast_fusion = f32[2,1024,256]{1,2,0:T(8,128)} fusion(f32[6,2,256,1024]{3,2,1,0:T(8,128)} %param.6, f32[6,256,256]{2,1,0:T(8,128)S(1)} %copy-done, f32[6]{0:T(128)S(1)} %get-tuple-element.52), kind=kOutput, calls=%fused_computation.13 | convolution fusion | flops 9664069632 | bytes 16252952 | tf_op jit(solution)/shard_map/scka,skr->car/dot_general | solution.py:24
  38.3 57.5 %all-reduce.9.cloned.1.call-done = (f32[256,1024]{1,0:T(8,128)}, f32[256,1024]{1,0:T(8,128)}, f32[256,1024]{1,0:T(8,128)}) async-done(((f32[256,1024]{1,0:T(8,128)}, f32[256,1024]{1,0:T(8,128)}, f32[256,1024]{1,0:T(8,128)}), (f32[256,1024]{1,0:T(8,128)}, f32[256,1024]{1,0:T(8,128)}, f32[256,1024]{1,0:T(8,128)})) %all-reduce.9.cloned.1.call-update) | async-done | bytes 3145744 | tf_op jit(solution)/shard_map/psum | solution.py:9
  95.9 140.0 %all-reduce.5.cloned.1.call-done = f32[2,1024,256]{1,2,0:T(8,128)} async-done(((f32[2,1024,256]{1,2,0:T(8,128)}), f32[2,1024,256]{1,2,0:T(8,128)}) %all-reduce.5.cloned.1.call-update) | async-done | bytes 2097168 | tf_op jit(solution)/shard_map/psum | solution.py:34
  235.9 1.0 dynamic-slice_subtract_fusion
  236.9 14.7 %all_gather.10 = f32[2,1024,32]{1,2,0:T(8,128)S(1)} all-gather(f32[2,256,32]{1,2,0:T(8,128)S(1)} %dynamic-slice_subtract_fusion), channel_id=1, replica_groups=mesh['rt'=8,'ct'=4] {'ct'}, dimensions={1}, use_global_device_ids=true | all-gather | bytes 327680 | tf_op jit(solution)/shard_map/all_gather | solution.py:37
  251.8 66.0 %all-gather.5.cloned.1.call-done = f32[1024,1024]{1,0:T(8,128)} async-done(((f32[256,1024]{1,0:T(8,128)}), f32[1024,1024]{1,0:T(8,128)}) %all-gather.5.cloned.1.call-update) | async-done | bytes 4194320 | tf_op jit(solution)/shard_map/all_gather | solution.py:40
  317.8 4.7 fusion.3
  322.6 22.5 %while.4 = (s32[]{:T(128)}, f32[1024,1024]{1,0:T(8,128)}, s32[8,2]{0,1:T(2,128)S(1)}, f32[8,128,128]{2,1,0:T(8,128)S(1)}, s32[]{:T(128)}) while((s32[]{:T(128)}, f32[1024,1024]{1,0:T(8,128)}, s32[8,2]{0,1:T(2,128)S(1)}, f32[8,128,128]{2,1,0:T(8,128)S(1)}, s32[]{:T(128)}) %tuple.49), condition=%wide.while_cond, body=%wide.while_body.sunk | while | flops 2 | bytes 131181 | solution.py:42
  323.2 2.2 bitcast_dynamic-update-slice_fusion.4
  326.1 2.2 bitcast_dynamic-update-slice_fusion.4
  328.9 2.2 bitcast_dynamic-update-slice_fusion.4
  331.7 2.2 bitcast_dynamic-update-slice_fusion.4
  334.5 2.2 bitcast_dynamic-update-slice_fusion.4
  337.3 2.2 bitcast_dynamic-update-slice_fusion.4
  340.2 2.2 bitcast_dynamic-update-slice_fusion.4
  343.0 2.1 bitcast_dynamic-update-slice_fusion.4
  345.1 78.6 %custom-call.4 = f32[8,128,128]{1,2,0:T(8,128)S(1)} custom-call(f32[8,128,128]{2,1,0:T(8,128)S(1)} %get-tuple-element.24), custom_call_target="InvertDiagBlocksLowerTriangular" | custom-call | tf_op jit(solution)/shard_map/triangular_solve/custom-call.1 | solution.py:42
  423.9 1.0 convolution_subtract_fusion.7
  425.2 1.1 convolution_subtract_fusion.6
  426.5 1.2 convolution_subtract_fusion.5
  427.9 1.2 convolution_subtract_fusion.4
  429.4 1.3 convolution_subtract_fusion.13
  431.0 1.3 convolution_subtract_fusion.12
  432.6 1.4 convolution_subtract_fusion.11
  434.3 1.4 fusion.67
  435.8 4.7 fusion.4
  440.5 24.2 %while.5 = (s32[]{:T(128)}, f32[1024,1024]{1,0:T(8,128)}, s32[8,2]{0,1:T(2,128)S(1)}, f32[8,128,128]{2,1,0:T(8,128)S(1)}, s32[]{:T(128)}) while((s32[]{:T(128)}, f32[1024,1024]{1,0:T(8,128)}, s32[8,2]{0,1:T(2,128)S(1)}, f32[8,128,128]{2,1,0:T(8,128)S(1)}, s32[]{:T(128)}) %tuple.66), condition=%wide.while_cond.clone, body=%wide.while_body.clone.sunk | while | flops 2 | bytes 131181 | solution.py:48
  441.2 2.3 bitcast_dynamic-update-slice_fusion.5
  444.2 2.3 bitcast_dynamic-update-slice_fusion.5
  447.3 2.3 bitcast_dynamic-update-slice_fusion.5
  450.3 2.3 bitcast_dynamic-update-slice_fusion.5
  453.3 2.3 bitcast_dynamic-update-slice_fusion.5
  456.4 2.3 bitcast_dynamic-update-slice_fusion.5
  459.4 2.3 bitcast_dynamic-update-slice_fusion.5
  462.4 2.3 bitcast_dynamic-update-slice_fusion.5
  464.7 78.6 %custom-call.5 = f32[8,128,128]{1,2,0:T(8,128)S(1)} custom-call(f32[8,128,128]{2,1,0:T(8,128)S(1)} %get-tuple-element.25), custom_call_target="InvertDiagBlocksLowerTriangular" | custom-call | tf_op jit(solution)/shard_map/triangular_solve/custom-call.1 | solution.py:48
  544.5 1.0 convolution_subtract_fusion.3
  545.7 1.1 convolution_subtract_fusion.2
  547.0 1.2 convolution_subtract_fusion.1
  548.4 1.2 convolution_subtract_fusion
  550.0 1.3 convolution_subtract_fusion.10
  551.5 1.3 convolution_subtract_fusion.9
  553.2 1.4 convolution_subtract_fusion.8
  (120 shorter events, 16.7 us)
Async XLA Ops:
  6.5 89.3 %all-reduce.9.cloned.1.call-start = ((), (), s32[]{:S(2)}) async-start(), calls=%async_computation.4 | async-start | bytes 6291456 | tf_op jit(solution)/shard_map/psum | solution.py:9
  21.4 1.9 copy-start
  23.1 212.8 %all-reduce.5.cloned.1.call-start = ((), (), s32[]{:S(2)}) async-start(), calls=%async_computation.1 | async-start | bytes 4194304 | tf_op jit(solution)/shard_map/psum | solution.py:34
  23.3 212.6 %copy-start.2 = (f32[2,256,32]{1,2,0:T(8,128)S(1)}, f32[2,256,32]{1,2,0:T(8,128)}, u32[]{:S(2)}) copy-start(f32[2,256,32]{1,2,0:T(8,128)} %param.9) | copy-start | bytes 196612
  38.2 279.6 %all-gather.5.cloned.1.call-start = ((), (), s32[]{:S(2)}) async-start(), calls=%async_computation.2 | async-start | bytes 5242880 | tf_op jit(solution)/shard_map/all_gather | solution.py:40
  95.8 339.9 %all-gather.3.cloned.1.call-start = ((), (), s32[]{:S(2)}) async-start(), calls=%async_computation | async-start | bytes 5242880 | tf_op jit(solution)/shard_map/all_gather | solution.py:39
  251.6 291.7 %all-reduce.7.cloned.1.call-start = ((), (), s32[]{:S(2)}) async-start(), calls=%async_computation.3 | async-start | bytes 262144 | tf_op jit(solution)/shard_map/psum | solution.py:47
  322.6 111.8 %copy-start.1 = (f32[256,1024]{1,0:T(8,128)S(1)}, f32[256,1024]{1,0:T(8,128)}, u32[]{:S(2)}) copy-start(f32[256,1024]{1,0:T(8,128)} %get-tuple-element.47) | copy-start | bytes 3145732
Sparse Core Ops, SparseCore 0:
  23.2 72.5 all-reduce.8
  102.0 133.8 all-reduce.4
  237.5 80.3 all-gather.4
  319.2 79.3 all-gather.2
  435.9 33.0 all-reduce.6
where the time goes:
time: 564 us; the launch traced here: 562 us
  waiting for transfers between devices  264 us (47%)
  other arithmetic  182 us (32%)
  local copies, waits for them, and re-layouts  47 us (8%)
  matrix products  36.6 us (6%)
  between operations  18 us (3%)
  blocking collectives  14.7 us (3%)
    psum x1, waiting for transfers between devices, shards(): total = lax.psum(partial_value, ('rt', 'ct'))  140 us
    another operation x3, other arithmetic, shards(): lax.linalg.triangular_solve(whole_zero, residual[0] - coupled, left_side=...  83.3 us
    another operation x2, other arithmetic, shards(): lax.linalg.triangular_solve(whole_one, residual[1], left_side=True, lower...  83.3 us
    all_gather x1, waiting for transfers between devices, shards(): lax.all_gather(tile_one, 'ct', axis=0, tiled=True)  66 us
    psum x1, waiting for transfers between devices, spread(): return lax.psum(jnp.where(mine, value, jnp.zeros_like(value)), axis)  57.5 us
    another operation x31, local copies, waits for them, and re-layouts, shards(): lax.linalg.triangular_solve(whole_zero, residual[0] - coupled, left_side=...  24.1 us
    another operation x28, local copies, waits for them, and re-layouts, shards(): lax.linalg.triangular_solve(whole_one, residual[1], left_side=True, lower...  22.4 us
    dot_general x1, matrix products, shards(): jnp.einsum('scka,skr->car', factor_rows, masked, precision=high)  14.9 us
  transfers between devices with their start and end apart: 5, of which 3 were waited for; matrix products, arithmetic and copies ran while one was open for 43% of the time, Pallas kernels for 0%

commit v1 on v0

--- a/solution.py
+++ b/solution.py
@@ -2,6 +2,11 @@
 import jax.numpy as jnp
 from jax import lax
 from jax.sharding import PartitionSpec as P
+
+
+def axis_by_axis(value_2, axis_one, axis_two):
+    partial = lax.psum(value_2, axis_one)
+    return lax.psum(partial, axis_two)
 
 
 def spread(value, axis, root):
@@ -31,7 +36,7 @@
     owner_one = jnp.argmax(slot_row == 1) // slot_count
     tile_zero = spread(diag_zero, "rt", owner_zero)
     tile_one, tile_lower = (spread(diag_one, "rt", owner_one), spread(lower_one, "rt", owner_one))
-    total = lax.psum(partial_value, ("rt", "ct"))
+    total = axis_by_axis(partial_value, "ct", "rt")
     rows_mine = lax.dynamic_slice_in_dim(total, offset, band, 1)
     mine = lax.dynamic_slice_in_dim(rows_mine, col_offset, columns, 2)
     residual = lax.all_gather(rhs - mine, "ct", axis=1, tiled=True)

time: 564 us -> 537 us (0.952)
  waiting for transfers between devices: 264 us -> 238 us
    psum x1, waiting for transfers between devices: 140 us -> 75 us  [axis_by_axis(): partial = lax.psum(value_2, axis_one)]
    psum x1, waiting for transfers between devices: 57.5 us -> 96.2 us  [spread(): return lax.psum(jnp.where(mine, value, jnp.zeros_like(value)), axis)]
  transfers between devices with their start and end apart: 5 -> 5, of which waited for: 3 -> 3; matrix products, arithmetic and copies ran while one was open for 43% -> 44% of each run, Pallas kernels for 0% -> 0%
where the time goes in v1:
time: 537 us; the launch traced here: 536 us
  waiting for transfers between devices  238 us (44%)
  other arithmetic  181 us (34%)
  local copies, waits for them, and re-layouts  46.8 us (9%)
  matrix products  37 us (7%)
  between operations  17.6 us (3%)
  blocking collectives  14.7 us (3%)
    psum x1, waiting for transfers between devices, spread(): return lax.psum(jnp.where(mine, value, jnp.zeros_like(value)), axis)  96.2 us
    another operation x3, other arithmetic, shards(): lax.linalg.triangular_solve(whole_zero, residual[0] - coupled, left_side=...  83.3 us
    another operation x2, other arithmetic, shards(): lax.linalg.triangular_solve(whole_one, residual[1], left_side=True, lower...  83.3 us
    psum x1, waiting for transfers between devices, axis_by_axis(): partial = lax.psum(value_2, axis_one)  75 us
    all_gather x1, waiting for transfers between devices, shards(): lax.all_gather(tile_one, 'ct', axis=0, tiled=True)  67.1 us
    another operation x31, local copies, waits for them, and re-layouts, shards(): lax.linalg.triangular_solve(whole_zero, residual[0] - coupled, left_side=...  24.1 us
    another operation x28, local copies, waits for them, and re-layouts, shards(): lax.linalg.triangular_solve(whole_one, residual[1], left_side=True, lower...  22.4 us
    dot_general x1, matrix products, shards(): jnp.einsum('scka,skr->car', factor_rows, masked, precision=high)  15.3 us
  transfers between devices with their start and end apart: 5, of which 3 were waited for; matrix products, arithmetic and copies ran while one was open for 44% of the time, Pallas kernels for 0%

profile of v1, /device:TPU:0, one launch (start us, length us, event | category | flops | bytes accessed | tf_op | source)
XLA Modules:
  0.0 535.6 jit_solution(10742743628016142090)
XLA Ops:
  6.5 0.7 compare_convert_fusion
  7.3 15.3 %convolution_bitcast_fusion = f32[2,1024,256]{1,2,0:T(8,128)} fusion(f32[6,2,256,1024]{3,2,1,0:T(8,128)} %param.6, f32[6,256,256]{2,1,0:T(8,128)} %param.8, f32[6]{0:T(128)S(1)} %get-tuple-element.53), kind=kOutput, calls=%fused_computation.13 | convolution fusion | flops 9664069632 | bytes 16252952 | tf_op jit(solution)/shard_map/scka,skr->car/dot_general | solution.py:29
  27.7 6.5 %fusion.2 = (f32[256,1024]{1,0:T(8,128)S(1)}, f32[256,1024]{1,0:T(8,128)S(1)}, f32[256,1024]{1,0:T(8,128)S(1)}) fusion(f32[6,2,256,1024]{3,2,1,0:T(8,128)} %param.6, pred[6]{0:T(512)(128)(4,1)S(1)} %get-tuple-element.54, pred[6]{0:T(512)(128)(4,1)S(1)} %get-tuple-element.55), kind=kLoop, calls=%fused_computation.9 | loop fusion | flops 8650752 | bytes 15728652 | tf_op jit(solution)/shard_map/reduce_sum | solution.py:34
  34.2 1.1 broadcast_select_fusion.2
  35.3 1.6 broadcast_select_fusion
  37.0 75.0 %all-reduce.5.cloned.1.call-done = f32[2,1024,256]{1,2,0:T(8,128)} async-done(((f32[2,1024,256]{1,2,0:T(8,128)}), f32[2,1024,256]{1,2,0:T(8,128)}) %all-reduce.5.cloned.1.call-update) | async-done | bytes 2097168 | tf_op jit(solution)/shard_map/psum | solution.py:8
  112.0 96.2 %all-reduce.9.cloned.1.call-done = (f32[256,1024]{1,0:T(8,128)}, f32[2,1024,256]{1,2,0:T(8,128)}, f32[256,1024]{1,0:T(8,128)}, f32[256,1024]{1,0:T(8,128)}) async-done(((f32[256,1024]{1,0:T(8,128)}, f32[2,1024,256]{1,2,0:T(8,128)}, f32[256,1024]{1,0:T(8,128)}, f32[256,1024]{1,0:T(8,128)}), (f32[256,1024]{1,0:T(8,128)}, f32[2,1024,256]{1,2,0:T(8,128)}, f32[256,1024]{1,0:T(8,128)}, ...) | async-done | bytes 5242896 | tf_op jit(solution)/shard_map/psum | solution.py:14
  208.4 1.0 dynamic-slice_subtract_fusion
  209.4 14.7 %all_gather.10 = f32[2,1024,32]{1,2,0:T(8,128)S(1)} all-gather(f32[2,256,32]{1,2,0:T(8,128)S(1)} %dynamic-slice_subtract_fusion), channel_id=1, replica_groups=mesh['rt'=8,'ct'=4] {'ct'}, dimensions={1}, use_global_device_ids=true | all-gather | bytes 327680 | tf_op jit(solution)/shard_map/all_gather | solution.py:42
  224.3 67.1 %all-gather.5.cloned.1.call-done = f32[1024,1024]{1,0:T(8,128)} async-done(((f32[256,1024]{1,0:T(8,128)}), f32[1024,1024]{1,0:T(8,128)}) %all-gather.5.cloned.1.call-update) | async-done | bytes 4194320 | tf_op jit(solution)/shard_map/all_gather | solution.py:45
  291.4 4.7 fusion.3
  296.2 22.5 %while.4 = (s32[]{:T(128)}, f32[1024,1024]{1,0:T(8,128)}, s32[8,2]{0,1:T(2,128)S(1)}, f32[8,128,128]{2,1,0:T(8,128)S(1)}, s32[]{:T(128)}) while((s32[]{:T(128)}, f32[1024,1024]{1,0:T(8,128)}, s32[8,2]{0,1:T(2,128)S(1)}, f32[8,128,128]{2,1,0:T(8,128)S(1)}, s32[]{:T(128)}) %tuple.49), condition=%wide.while_cond, body=%wide.while_body.sunk | while | flops 2 | bytes 131181 | solution.py:47
  296.8 2.2 bitcast_dynamic-update-slice_fusion.4
  299.6 2.2 bitcast_dynamic-update-slice_fusion.4
  302.5 2.2 bitcast_dynamic-update-slice_fusion.4
  305.3 2.2 bitcast_dynamic-update-slice_fusion.4
  308.1 2.2 bitcast_dynamic-update-slice_fusion.4
  310.9 2.2 bitcast_dynamic-update-slice_fusion.4
  313.7 2.2 bitcast_dynamic-update-slice_fusion.4
  316.6 2.1 bitcast_dynamic-update-slice_fusion.4
  318.7 78.6 %custom-call.4 = f32[8,128,128]{1,2,0:T(8,128)S(1)} custom-call(f32[8,128,128]{2,1,0:T(8,128)S(1)} %get-tuple-element.24), custom_call_target="InvertDiagBlocksLowerTriangular" | custom-call | tf_op jit(solution)/shard_map/triangular_solve/custom-call.1 | solution.py:47
  397.5 1.0 convolution_subtract_fusion.7
  398.7 1.1 convolution_subtract_fusion.6
  400.1 1.2 convolution_subtract_fusion.5
  401.5 1.2 convolution_subtract_fusion.4
  403.0 1.3 convolution_subtract_fusion.13
  404.6 1.3 convolution_subtract_fusion.12
  406.2 1.4 convolution_subtract_fusion.11
  407.9 1.4 fusion.67
  409.3 4.7 fusion.4
  414.1 24.2 %while.5 = (s32[]{:T(128)}, f32[1024,1024]{1,0:T(8,128)}, s32[8,2]{0,1:T(2,128)S(1)}, f32[8,128,128]{2,1,0:T(8,128)S(1)}, s32[]{:T(128)}) while((s32[]{:T(128)}, f32[1024,1024]{1,0:T(8,128)}, s32[8,2]{0,1:T(2,128)S(1)}, f32[8,128,128]{2,1,0:T(8,128)S(1)}, s32[]{:T(128)}) %tuple.66), condition=%wide.while_cond.clone, body=%wide.while_body.clone.sunk | while | flops 2 | bytes 131181 | solution.py:53
  414.8 2.3 bitcast_dynamic-update-slice_fusion.5
  417.8 2.3 bitcast_dynamic-update-slice_fusion.5
  420.9 2.3 bitcast_dynamic-update-slice_fusion.5
  423.9 2.3 bitcast_dynamic-update-slice_fusion.5
  426.9 2.3 bitcast_dynamic-update-slice_fusion.5
  429.9 2.3 bitcast_dynamic-update-slice_fusion.5
  433.0 2.3 bitcast_dynamic-update-slice_fusion.5
  436.0 2.3 bitcast_dynamic-update-slice_fusion.5
  438.3 78.6 %custom-call.5 = f32[8,128,128]{1,2,0:T(8,128)S(1)} custom-call(f32[8,128,128]{2,1,0:T(8,128)S(1)} %get-tuple-element.25), custom_call_target="InvertDiagBlocksLowerTriangular" | custom-call | tf_op jit(solution)/shard_map/triangular_solve/custom-call.1 | solution.py:53
  516.9 0.9 fusion.20
  518.1 1.0 convolution_subtract_fusion.3
  519.3 1.1 convolution_subtract_fusion.2
  520.6 1.2 convolution_subtract_fusion.1
  522.0 1.2 convolution_subtract_fusion
  523.5 1.3 convolution_subtract_fusion.10
  525.1 1.3 convolution_subtract_fusion.9
  526.7 1.4 convolution_subtract_fusion.8
  (120 shorter events, 16.2 us)
Async XLA Ops:
  6.5 105.4 %all-reduce.5.cloned.1.call-start = ((), (), s32[]{:S(2)}) async-start(), calls=%async_computation.1 | async-start | bytes 4194304 | tf_op jit(solution)/shard_map/psum | solution.py:8
  7.3 15.4 %copy-start.2 = (s32[48]{0:T(128)S(1)}, s32[48]{0:T(128)}, u32[]{:S(2)}) copy-start(s32[48]{0:T(128)} %param.7) | copy-start | bytes 580
  22.6 185.7 %all-reduce.9.cloned.1.call-start = ((), (), s32[]{:S(2)}) async-start(), calls=%async_computation.4 | async-start | bytes 10485760 | tf_op jit(solution)/shard_map/psum | solution.py:14
  37.0 171.4 %copy-start.1 = (f32[2,256,32]{1,2,0:T(8,128)S(1)}, f32[2,256,32]{1,2,0:T(8,128)}, u32[]{:S(2)}) copy-start(f32[2,256,32]{1,2,0:T(8,128)} %param.9) | copy-start | bytes 196612
  112.0 179.4 %all-gather.5.cloned.1.call-start = ((), (), s32[]{:S(2)}) async-start(), calls=%async_computation.2 | async-start | bytes 5242880 | tf_op jit(solution)/shard_map/all_gather | solution.py:45
  208.3 201.1 %all-gather.3.cloned.1.call-start = ((), (), s32[]{:S(2)}) async-start(), calls=%async_computation | async-start | bytes 5242880 | tf_op jit(solution)/shard_map/all_gather | solution.py:44
  224.1 292.8 %all-reduce.7.cloned.1.call-start = ((), (), s32[]{:S(2)}) async-start(), calls=%async_computation.3 | async-start | bytes 262144 | tf_op jit(solution)/shard_map/psum | solution.py:52
  296.1 111.8 %copy-start = (f32[256,1024]{1,0:T(8,128)S(1)}, f32[256,1024]{1,0:T(8,128)}, u32[]{:S(2)}) copy-start(f32[256,1024]{1,0:T(8,128)} %get-tuple-element.48) | copy-start | bytes 3145732
Sparse Core Ops, SparseCore 0:
  22.7 89.1 all-reduce.4
  116.1 92.1 all-reduce.8
  209.8 81.5 all-gather.4
  292.8 78.8 all-gather.2
  409.4 32.4 all-reduce.6
